TPU v7x, 512 devices: a whole 4x8x8 slice. The times are simulated.
512 devices in a mesh: dp: 64 (over y, z_hi, core), tensor: 8 (over x, z_lo).
Axes of the slice: x: 4, y: 8, z: 8 (z_hi: 4, z_lo: 2; z = z_hi * 2 + z_lo), core: 2. Of those that a mesh axis runs over, the one named last changes fastest.
Arguments:
- inputs: float32 [16384, 1024], P('dp', 'tensor'), may hold values from -16 to 16
- cotangent: float32 [16384, 1024], P('dp', 'tensor'), may hold values from -0.12 to 0.12
- gate_weight: float32 [1024, 4096], P('dp', 'tensor'), may hold values from -0.1875 to 0.1875
- up_weight: float32 [1024, 4096], P('dp', 'tensor'), may hold values from -0.1875 to 0.1875
- down_weight: float32 [1024, 4096], P('dp', 'tensor'), may hold values from -0.09375 to 0.09375
- gate_first: float32 [1024, 4096], P('dp', 'tensor'), may hold values from -6 to 6
- gate_second: float32 [1024, 4096], P('dp', 'tensor'), may hold values from 0.5 to 4
- up_first: float32 [1024, 4096], P('dp', 'tensor'), may hold values from -6 to 6
- up_second: float32 [1024, 4096], P('dp', 'tensor'), may hold values from 0.5 to 4
Outputs:
- gate_new: float32 [1024, 4096], P('dp', 'tensor')
- gate_first_new: float32 [1024, 4096], P('dp', 'tensor')
- gate_second_new: float32 [1024, 4096], P('dp', 'tensor')
- up_new: float32 [1024, 4096], P('dp', 'tensor')
- up_first_new: float32 [1024, 4096], P('dp', 'tensor')
- up_second_new: float32 [1024, 4096], P('dp', 'tensor')
All inputs are finite; a program needn't handle non-finite values.
Results may differ from a plain program's by a relative error of at most 0.00005.
Values sent between devices are 32-bit elements; how exact they have to be, the bound alone decides.
A program may use at most 64 MiB of HBM per device.

v0:
```python
import jax
import jax.numpy as jnp
from jax import lax
from jax.sharding import PartitionSpec as P

STEP = 100


def adam_update(weight, first, second, grad):
    first_new = 0.9 * first + 0.1 * grad
    second_new = 0.95 * second + 0.05 * grad * grad
    first_hat = first_new / (1.0 - 0.9**STEP)
    second_hat = second_new / (1.0 - 0.95**STEP)
    weight_new = weight - 0.003 * first_hat / (jnp.sqrt(second_hat) + 1e-08)
    return (weight_new, first_new, second_new)


def contract(left, piece):
    return jnp.dot(left, piece, precision=lax.Precision.HIGHEST, preferred_element_type=jnp.float32)


def local(
    inputs,
    cotangent,
    gate_weight,
    up_weight,
    down_weight,
    gate_first,
    gate_second,
    up_first,
    up_second,
):
    rows_full, cot_full = (
        lax.all_gather(inputs, "tensor", axis=1, tiled=True),
        lax.all_gather(cotangent, "tensor", axis=1, tiled=True),
    )
    gate_sum = contract(rows_full, lax.all_gather(gate_weight, "dp", axis=0, tiled=True))
    lift_sum = contract(rows_full, lax.all_gather(up_weight, "dp", axis=0, tiled=True))
    back_sum = contract(cot_full, lax.all_gather(down_weight, "dp", axis=0, tiled=True))
    sigmoid_gate = jax.nn.sigmoid(gate_sum)
    gate_rows = back_sum * lift_sum * sigmoid_gate * (1.0 + gate_sum * (1.0 - sigmoid_gate))
    lift_rows = back_sum * gate_sum * sigmoid_gate

    def make_term(grad_rows):
        return lax.dot_general(
            rows_full,
            grad_rows,
            (((0,), (0,)), ((), ())),
            precision=lax.Precision.HIGHEST,
            preferred_element_type=jnp.float32,
        )

    gate_grad = lax.psum_scatter(make_term(gate_rows), "dp", scatter_dimension=0, tiled=True)
    lift_grad = lax.psum_scatter(make_term(lift_rows), "dp", scatter_dimension=0, tiled=True)
    gate_new, gate_first_new, gate_second_new = adam_update(
        gate_weight, gate_first, gate_second, gate_grad
    )
    up_new, up_first_new, up_second_new = adam_update(up_weight, up_first, up_second, lift_grad)
    return (gate_new, gate_first_new, gate_second_new, up_new, up_first_new, up_second_new)


def solution(mesh):
    in_specs = (
        P("dp", "tensor"),
        P("dp", "tensor"),
        P("dp", "tensor"),
        P("dp", "tensor"),
        P("dp", "tensor"),
        P("dp", "tensor"),
        P("dp", "tensor"),
        P("dp", "tensor"),
        P("dp", "tensor"),
    )
    out_specs = (
        P("dp", "tensor"),
        P("dp", "tensor"),
        P("dp", "tensor"),
        P("dp", "tensor"),
        P("dp", "tensor"),
        P("dp", "tensor"),
    )
    return jax.shard_map(local, mesh=mesh, in_specs=in_specs, out_specs=out_specs, check_vma=False)
```

profile of v0, /device:TPU:2, one launch (start us, length us, event | category | flops | bytes accessed | tf_op | source)
XLA Modules:
  0.0 683.1 jit_solution(2127603420906008118)
XLA Ops:
  7.2 0.0 all-gather.6.cloned.1.call-start
  7.2 0.7 all-gather.6.cloned.1.call-update
  7.9 0.0 all-gather.8.cloned.1.call-start
  7.9 0.7 all-gather.8.cloned.1.call-update
  8.6 0.0 all-gather.10.cloned.1.call-start
  8.7 0.7 all-gather.10.cloned.1.call-update
  9.4 0.0 all-gather.14.cloned.1.call-start
  9.4 0.5 all-gather.14.cloned.1.call-update
  10.0 0.0 all-gather.12.cloned.1.call-start
  10.0 0.5 all-gather.12.cloned.1.call-update
  10.5 0.0 reduce-scatter.9.cloned.1.call-start
  10.6 49.5 %all-gather.6.cloned.1.call-done = f32[256,1024]{1,0:T(8,128)} async-done(((f32[256,128]{1,0:T(8,128)}), f32[256,1024]{1,0:T(8,128)}) %all-gather.6.cloned.1.call-update) | async-done | bytes 1048592 | tf_op jit(solution)/shard_map/all_gather | solution.py:35
  60.1 89.3 %all-gather.8.cloned.1.call-done = f32[1024,512]{1,0:T(8,128)} async-done(((f32[16,512]{1,0:T(8,128)}), f32[1024,512]{1,0:T(8,128)}) %all-gather.8.cloned.1.call-update) | async-done | bytes 2097168 | tf_op jit(solution)/shard_map/all_gather | solution.py:39
  149.4 4.7 fusion.10
  154.1 39.5 %all-gather.10.cloned.1.call-done = f32[256,1024]{1,0:T(8,128)} async-done(((f32[256,128]{1,0:T(8,128)}), f32[256,1024]{1,0:T(8,128)}) %all-gather.10.cloned.1.call-update) | async-done | bytes 1048592 | tf_op jit(solution)/shard_map/all_gather | solution.py:34
  193.7 89.2 %all-gather.14.cloned.1.call-done = f32[1024,512]{1,0:T(8,128)} async-done(((f32[16,512]{1,0:T(8,128)}), f32[1024,512]{1,0:T(8,128)}) %all-gather.14.cloned.1.call-update) | async-done | bytes 2097168 | tf_op jit(solution)/shard_map/all_gather | solution.py:37
  282.8 3.9 fusion.11
  286.7 0.8 copy-done.3
  287.6 2.0 convolution_bitcast_fusion
  289.5 1.8 copy.55
  291.3 0.0 reduce-scatter.9.cloned.1.call-update
  291.4 0.0 reduce-scatter.7.cloned.1.call-start
  291.4 76.3 %all-gather.12.cloned.1.call-done = f32[1024,512]{1,0:T(8,128)} async-done(((f32[16,512]{1,0:T(8,128)}), f32[1024,512]{1,0:T(8,128)}) %all-gather.12.cloned.1.call-update) | async-done | bytes 2097168 | tf_op jit(solution)/shard_map/all_gather | solution.py:38
  367.7 3.6 fusion.1
  371.4 1.9 convolution_bitcast_fusion.1
  373.2 1.8 copy.53
  375.1 0.0 copy-start.9
  375.1 0.0 reduce-scatter.7.cloned.1.call-update
  375.1 146.2 %reduce-scatter.9.cloned.1.call-done = f32[16,512]{1,0:T(8,128)} async-done(((f32[1024,512]{1,0:T(8,128)}), f32[16,512]{1,0:T(8,128)}) %reduce-scatter.9.cloned.1.call-update) | async-done | bytes 32784 | tf_op jit(solution)/shard_map/reduce_scatter | solution.py:54
  521.4 1.4 divide_subtract_fusion
  522.8 152.1 %reduce-scatter.7.cloned.1.call-done = f32[16,512]{1,0:T(8,128)} async-done(((f32[1024,512]{1,0:T(8,128)}), f32[16,512]{1,0:T(8,128)}) %reduce-scatter.7.cloned.1.call-update) | async-done | bytes 32784 | tf_op jit(solution)/shard_map/reduce_scatter | solution.py:53
  674.9 1.4 divide_subtract_fusion.1
  (20 shorter events, 0.0 us)
Async XLA Ops:
  7.2 52.9 %all-gather.6.cloned.1.call-start = ((), (), s32[]{:S(2)}) async-start(), calls=%async_computation.2 | async-start | bytes 1179648 | tf_op jit(solution)/shard_map/all_gather | solution.py:35
  7.9 141.5 %all-gather.8.cloned.1.call-start = ((), (), s32[]{:S(2)}) async-start(), calls=%async_computation.3 | async-start | bytes 2129920 | tf_op jit(solution)/shard_map/all_gather | solution.py:39
  8.6 185.0 %all-gather.10.cloned.1.call-start = ((), (), s32[]{:S(2)}) async-start(), calls=%async_computation.4 | async-start | bytes 1179648 | tf_op jit(solution)/shard_map/all_gather | solution.py:34
  9.4 273.4 %all-gather.14.cloned.1.call-start = ((), (), s32[]{:S(2)}) async-start(), calls=%async_computation.6 | async-start | bytes 2129920 | tf_op jit(solution)/shard_map/all_gather | solution.py:37
  10.0 357.8 %all-gather.12.cloned.1.call-start = ((), (), s32[]{:S(2)}) async-start(), calls=%async_computation.5 | async-start | bytes 2129920 | tf_op jit(solution)/shard_map/all_gather | solution.py:38
  10.5 510.8 %reduce-scatter.9.cloned.1.call-start = ((), (), s32[]{:S(2)}) async-start(), calls=%async_computation.8 | async-start | bytes 2129920 | tf_op jit(solution)/shard_map/reduce_scatter | solution.py:54
  193.7 93.9 %copy-start = (f32[256,1024]{1,0:T(8,128)S(1)}, f32[256,1024]{1,0:T(8,128)}, u32[]{:S(2)}) copy-start(f32[256,1024]{1,0:T(8,128)} %all-gather.10.cloned.1.call-done) | copy-start | bytes 3145732
  282.8 4.7 copy-start.1
  286.7 0.8 copy-start.3
  291.3 76.4 %copy-start.2 = (f32[256,512]{1,0:T(8,128)S(1)}, f32[256,512]{1,0:T(8,128)}, u32[]{:S(2)}) copy-start(f32[256,512]{1,0:T(8,128)} %fusion.10) | copy-start | bytes 1572868
  291.3 76.4 %copy-start.4 = (f32[256,512]{1,0:T(8,128)S(1)}, f32[256,512]{1,0:T(8,128)}, u32[]{:S(2)}) copy-start(f32[256,512]{1,0:T(8,128)} %copy-done.3) | copy-start | bytes 1572868
  291.4 383.5 %reduce-scatter.7.cloned.1.call-start = ((), (), s32[]{:S(2)}) async-start(), calls=%async_computation.7 | async-start | bytes 2129920 | tf_op jit(solution)/shard_map/reduce_scatter | solution.py:53
  375.1 146.3 %copy-start.5 = (f32[16,512]{1,0:T(8,128)S(1)}, f32[16,512]{1,0:T(8,128)}, u32[]{:S(2)}) copy-start(f32[16,512]{1,0:T(8,128)} %param.12) | copy-start | bytes 98308
  375.1 146.3 %copy-start.7 = (f32[16,512]{1,0:T(8,128)S(1)}, f32[16,512]{1,0:T(8,128)}, u32[]{:S(2)}) copy-start(f32[16,512]{1,0:T(8,128)} %param.16) | copy-start | bytes 98308
  375.1 146.3 %copy-start.8 = (f32[16,512]{1,0:T(8,128)S(1)}, f32[16,512]{1,0:T(8,128)}, u32[]{:S(2)}) copy-start(f32[16,512]{1,0:T(8,128)} %param.17) | copy-start | bytes 98308
  375.1 299.8 %copy-start.6 = (f32[16,512]{1,0:T(8,128)S(1)}, f32[16,512]{1,0:T(8,128)}, u32[]{:S(2)}) copy-start(f32[16,512]{1,0:T(8,128)} %param.11) | copy-start | bytes 98308
  375.1 299.8 %copy-start.9 = (f32[16,512]{1,0:T(8,128)S(1)}, f32[16,512]{1,0:T(8,128)}, u32[]{:S(2)}) copy-start(f32[16,512]{1,0:T(8,128)} %param.14) | copy-start | bytes 98308
  375.1 299.8 %copy-start.10 = (f32[16,512]{1,0:T(8,128)S(1)}, f32[16,512]{1,0:T(8,128)}, u32[]{:S(2)}) copy-start(f32[16,512]{1,0:T(8,128)} %param.15) | copy-start | bytes 98308
Sparse Core Ops, SparseCore 0:
  10.0 50.0 all-gather.5
  63.4 85.9 all-gather.7
  151.4 42.1 all-gather.9
  196.8 85.9 all-gather.13
  286.0 81.6 all-gather.11
  372.2 149.1 reduce-scatter.8
  526.0 148.8 reduce-scatter.6
where the time goes:
time: 683 us
  waiting for transfers between devices  645 us (94%)
  matrix products  16.1 us (2%)
  between operations  14.2 us (2%)
    reduce_scatter x1, waiting for transfers between devices, local(): lax.psum_scatter(make_term(gate_rows), 'dp', scatter_dimension=0, tiled=T...  152 us
    reduce_scatter x1, waiting for transfers between devices, local(): lax.psum_scatter(make_term(lift_rows), 'dp', scatter_dimension=0, tiled=T...  146 us
    all_gather x1, waiting for transfers between devices, local(): lax.all_gather(down_weight, 'dp', axis=0, tiled=True)  89.3 us
    all_gather x1, waiting for transfers between devices, local(): lax.all_gather(gate_weight, 'dp', axis=0, tiled=True)  89.2 us
    all_gather x1, waiting for transfers between devices, local(): lax.all_gather(up_weight, 'dp', axis=0, tiled=True)  76.3 us
    all_gather x1, waiting for transfers between devices, local(): lax.all_gather(cotangent, 'tensor', axis=1, tiled=True)  49.5 us
    all_gather x1, waiting for transfers between devices, local(): lax.all_gather(inputs, 'tensor', axis=1, tiled=True)  39.5 us
  transfers between devices with their start and end apart: 7, of which 7 were waited for; matrix products, arithmetic and copies ran while one was open for 3% of the time, Pallas kernels for 0%

commit v1 on v0

--- a/solution.py
+++ b/solution.py
@@ -30,8 +30,15 @@
     up_first,
     up_second,
 ):
+
+    def lift_threads(slab_in, mesh_name, array_dim):
+        odd = lax.all_to_all(
+            jnp.stack([slab_in for _ in range(lax.axis_size(mesh_name))], 0), mesh_name, 0, 0
+        )
+        return jnp.concatenate(odd, array_dim)
+
     rows_full, cot_full = (
-        lax.all_gather(inputs, "tensor", axis=1, tiled=True),
+        lift_threads(inputs, "tensor", 1),
         lax.all_gather(cotangent, "tensor", axis=1, tiled=True),
     )
     gate_sum = contract(rows_full, lax.all_gather(gate_weight, "dp", axis=0, tiled=True))

time: 683 us -> 640 us (0.937)
  waiting for transfers between devices: 645 us -> 578 us
  blocking collectives: 0 us -> 20.4 us
    all_gather x1 -> x0, waiting for transfers between devices: 39.5 us -> none  [local(): lax.all_gather(inputs, 'tensor', axis=1, tiled=True)]
    all_to_all x0 -> x1, blocking collectives: none -> 20.4 us  [lift_threads(): lax.all_to_all(jnp.stack([slab_in for _ in range(lax.axis_size(mesh_name)...]
    all_gather x1, waiting for transfers between devices: 89.2 us -> 69.4 us  [local(): lax.all_gather(gate_weight, 'dp', axis=0, tiled=True)]
    reduce_scatter x1, waiting for transfers between devices: 152 us -> 142 us  [local(): lax.psum_scatter(make_term(gate_rows), 'dp', scatter_dimension=0, tiled=T...]
    all_gather x1, waiting for transfers between devices: 49.5 us -> 40.7 us  [local(): lax.all_gather(cotangent, 'tensor', axis=1, tiled=True)]
  transfers between devices with their start and end apart: 7 -> 6, of which waited for: 7 -> 6; matrix products, arithmetic and copies ran while one was open for 3% -> 3% of each run, Pallas kernels for 0% -> 0%
where the time goes in v1:
time: 640 us; the launch traced here: 639 us
  waiting for transfers between devices  578 us (90%)
  blocking collectives  20.4 us (3%)
  matrix products  19.3 us (3%)
  between operations  14.2 us (2%)
    reduce_scatter x1, waiting for transfers between devices, local(): lax.psum_scatter(make_term(lift_rows), 'dp', scatter_dimension=0, tiled=T...  152 us
    reduce_scatter x1, waiting for transfers between devices, local(): lax.psum_scatter(make_term(gate_rows), 'dp', scatter_dimension=0, tiled=T...  142 us
    all_gather x1, waiting for transfers between devices, local(): lax.all_gather(down_weight, 'dp', axis=0, tiled=True)  89.3 us
    all_gather x1, waiting for transfers between devices, local(): lax.all_gather(up_weight, 'dp', axis=0, tiled=True)  81 us
    all_gather x1, waiting for transfers between devices, local(): lax.all_gather(gate_weight, 'dp', axis=0, tiled=True)  69.4 us
    all_gather x1, waiting for transfers between devices, local(): lax.all_gather(cotangent, 'tensor', axis=1, tiled=True)  40.7 us
    all_to_all x1, blocking collectives, lift_threads(): lax.all_to_all(jnp.stack([slab_in for _ in range(lax.axis_size(mesh_name)...  20.4 us
  transfers between devices with their start and end apart: 6, of which 6 were waited for; matrix products, arithmetic and copies ran while one was open for 3% of the time, Pallas kernels for 0%

profile of v1, /device:TPU:2, one launch (start us, length us, event | category | flops | bytes accessed | tf_op | source)
XLA Modules:
  0.0 639.4 jit_solution(4147681388615940851)
XLA Ops:
  7.2 0.0 all-gather.11.cloned.1.call-start
  7.2 0.7 all-gather.11.cloned.1.call-update
  7.9 0.0 all-gather.5.cloned.1.call-start
  7.9 0.7 all-gather.5.cloned.1.call-update
  8.6 0.0 all-gather.7.cloned.1.call-start
  8.7 0.7 all-gather.7.cloned.1.call-update
  9.4 0.0 all-gather.9.cloned.1.call-start
  9.4 0.5 all-gather.9.cloned.1.call-update
  10.0 0.0 reduce-scatter.7.cloned.1.call-start
  10.0 1.0 copy.65
  11.0 0.1 stack.2
  11.1 20.4 %all_to_all.5 = f32[8,256,128]{1,2,0:T(8,128)S(1)} all-to-all(f32[8,256,128]{1,2,0:T(8,128)S(1)} %stack.2), channel_id=1, replica_groups=mesh['dp'=64,'tensor'=8] {'tensor'}, dimensions={0} | all-to-all | bytes 2097152 | tf_op jit(solution)/shard_map/all_to_all | solution.py:35
  31.5 69.4 %all-gather.11.cloned.1.call-done = f32[1024,512]{1,0:T(8,128)} async-done(((f32[16,512]{1,0:T(8,128)}), f32[1024,512]{1,0:T(8,128)}) %all-gather.11.cloned.1.call-update) | async-done | bytes 2097168 | tf_op jit(solution)/shard_map/all_gather | solution.py:44
  100.9 3.5 fusion.11
  104.4 40.7 %all-gather.5.cloned.1.call-done = f32[256,1024]{1,0:T(8,128)} async-done(((f32[256,128]{1,0:T(8,128)}), f32[256,1024]{1,0:T(8,128)}) %all-gather.5.cloned.1.call-update) | async-done | bytes 1048592 | tf_op jit(solution)/shard_map/all_gather | solution.py:42
  145.2 89.3 %all-gather.7.cloned.1.call-done = f32[1024,512]{1,0:T(8,128)} async-done(((f32[16,512]{1,0:T(8,128)}), f32[1024,512]{1,0:T(8,128)}) %all-gather.7.cloned.1.call-update) | async-done | bytes 2097168 | tf_op jit(solution)/shard_map/all_gather | solution.py:46
  234.5 3.8 fusion.10
  238.3 81.0 %all-gather.9.cloned.1.call-done = f32[1024,512]{1,0:T(8,128)} async-done(((f32[16,512]{1,0:T(8,128)}), f32[1024,512]{1,0:T(8,128)}) %all-gather.9.cloned.1.call-update) | async-done | bytes 2097168 | tf_op jit(solution)/shard_map/all_gather | solution.py:45
  319.4 3.6 fusion.1
  323.0 3.6 convolution_bitcast_fusion.1
  326.6 1.8 copy.72
  328.4 0.0 reduce-scatter.7.cloned.1.call-update
  328.4 0.2 reduce-scatter.9.cloned.1.call-start
  328.6 4.7 convolution_bitcast_fusion
  333.4 1.8 copy.74
  335.2 0.0 copy-start.6
  335.2 0.0 copy-start.7
  335.2 0.0 reduce-scatter.9.cloned.1.call-update
  335.2 142.5 %reduce-scatter.7.cloned.1.call-done = f32[16,512]{1,0:T(8,128)} async-done(((f32[1024,512]{1,0:T(8,128)}), f32[16,512]{1,0:T(8,128)}) %reduce-scatter.7.cloned.1.call-update) | async-done | bytes 32784 | tf_op jit(solution)/shard_map/reduce_scatter | solution.py:60
  477.7 1.4 divide_subtract_fusion.1
  479.1 152.0 %reduce-scatter.9.cloned.1.call-done = f32[16,512]{1,0:T(8,128)} async-done(((f32[1024,512]{1,0:T(8,128)}), f32[16,512]{1,0:T(8,128)}) %reduce-scatter.9.cloned.1.call-update) | async-done | bytes 32784 | tf_op jit(solution)/shard_map/reduce_scatter | solution.py:61
  631.2 1.4 divide_subtract_fusion
  (14 shorter events, 0.0 us)
Async XLA Ops:
  7.2 93.7 %all-gather.11.cloned.1.call-start = ((), (), s32[]{:S(2)}) async-start(), calls=%async_computation.6 | async-start | bytes 2129920 | tf_op jit(solution)/shard_map/all_gather | solution.py:44
  7.9 137.3 %all-gather.5.cloned.1.call-start = ((), (), s32[]{:S(2)}) async-start(), calls=%async_computation.3 | async-start | bytes 1179648 | tf_op jit(solution)/shard_map/all_gather | solution.py:42
  8.6 225.8 %all-gather.7.cloned.1.call-start = ((), (), s32[]{:S(2)}) async-start(), calls=%async_computation.4 | async-start | bytes 2129920 | tf_op jit(solution)/shard_map/all_gather | solution.py:46
  9.4 310.0 %all-gather.9.cloned.1.call-start = ((), (), s32[]{:S(2)}) async-start(), calls=%async_computation.5 | async-start | bytes 2129920 | tf_op jit(solution)/shard_map/all_gather | solution.py:45
  10.0 467.7 %reduce-scatter.7.cloned.1.call-start = ((), (), s32[]{:S(2)}) async-start(), calls=%async_computation.7 | async-start | bytes 2129920 | tf_op jit(solution)/shard_map/reduce_scatter | solution.py:60
  104.4 214.9 %copy-start = (f32[256,512]{1,0:T(8,128)}, f32[256,512]{1,0:T(8,128)S(1)}, u32[]{:S(2)}) copy-start(f32[256,512]{1,0:T(8,128)S(1)} %fusion.11) | copy-start | bytes 1572868
  238.3 81.0 %copy-start.1 = (f32[256,512]{1,0:T(8,128)}, f32[256,512]{1,0:T(8,128)S(1)}, u32[]{:S(2)}) copy-start(f32[256,512]{1,0:T(8,128)S(1)} %fusion.10) | copy-start | bytes 1572868
  328.4 302.7 %reduce-scatter.9.cloned.1.call-start = ((), (), s32[]{:S(2)}) async-start(), calls=%async_computation.8 | async-start | bytes 2129920 | tf_op jit(solution)/shard_map/reduce_scatter | solution.py:61
  335.2 142.5 %copy-start.2 = (f32[16,512]{1,0:T(8,128)S(1)}, f32[16,512]{1,0:T(8,128)}, u32[]{:S(2)}) copy-start(f32[16,512]{1,0:T(8,128)} %param.11) | copy-start | bytes 98308
  335.2 142.5 %copy-start.4 = (f32[16,512]{1,0:T(8,128)S(1)}, f32[16,512]{1,0:T(8,128)}, u32[]{:S(2)}) copy-start(f32[16,512]{1,0:T(8,128)} %param.14) | copy-start | bytes 98308
  335.2 142.5 %copy-start.5 = (f32[16,512]{1,0:T(8,128)S(1)}, f32[16,512]{1,0:T(8,128)}, u32[]{:S(2)}) copy-start(f32[16,512]{1,0:T(8,128)} %param.15) | copy-start | bytes 98308
  335.2 296.0 %copy-start.3 = (f32[16,512]{1,0:T(8,128)S(1)}, f32[16,512]{1,0:T(8,128)}, u32[]{:S(2)}) copy-start(f32[16,512]{1,0:T(8,128)} %param.12) | copy-start | bytes 98308
  335.2 296.0 %copy-start.6 = (f32[16,512]{1,0:T(8,128)S(1)}, f32[16,512]{1,0:T(8,128)}, u32[]{:S(2)}) copy-start(f32[16,512]{1,0:T(8,128)} %param.16) | copy-start | bytes 98308
  335.2 296.0 %copy-start.7 = (f32[16,512]{1,0:T(8,128)S(1)}, f32[16,512]{1,0:T(8,128)}, u32[]{:S(2)}) copy-start(f32[16,512]{1,0:T(8,128)} %param.17) | copy-start | bytes 98308
Sparse Core Ops, SparseCore 0:
  11.3 89.5 all-gather.10
  102.9 42.1 all-gather.4
  148.5 85.9 all-gather.6
  237.6 81.6 all-gather.8
  328.5 149.1 reduce-scatter.6
  482.2 148.9 reduce-scatter.8
